TPU v7x, 32 devices: a whole 2x2x4 slice. The times are simulated.
32 devices in a mesh: items: 16 (over z, y, core), seq: 2 (over x).
Axes of the slice: x: 2, y: 2, z: 4, core: 2. Of those that a mesh axis runs over, the one named last changes fastest.
Arguments:
- tokens: bfloat16 [16, 1280, 1024], P('items', 'seq'), may hold values from -6 to 6
- cotangent: bfloat16 [16, 1280, 1024], P('items', 'seq'), may hold values from -6 to 6
- prompt_len: int32 [16], P('items'), may hold values from 150 to 600
- section_ids: int32 [16], P('items'), may hold values from 0 to 7
- section_table: bfloat16 [8, 1024], replicated, may hold values from -6 to 6
- w_query: bfloat16 [1024, 1024], P('items'), may hold values from -0.1875 to 0.1875
- w_key: bfloat16 [1024, 1024], P('items'), may hold values from -0.1875 to 0.1875
- w_value: bfloat16 [1024, 1024], P('items'), may hold values from -0.1875 to 0.1875
- w_out: bfloat16 [1024, 1024], P('items'), may hold values from -4 to 4
- w_up: bfloat16 [1024, 4096], P('items'), may hold values from -0.1875 to 0.1875
- w_down: bfloat16 [4096, 1024], P('items'), may hold values from -0.09375 to 0.09375
- w_ada_one: bfloat16 [1024, 2048], P('items'), may hold values from -0.09375 to 0.09375
- w_ada_two: bfloat16 [1024, 2048], P('items'), may hold values from -0.09375 to 0.09375
Outputs:
- layer_out: bfloat16 [16, 1280, 1024], P('items', 'seq')
- input_grad: float32 [16, 1280, 1024], P('items', 'seq')
- grad_query: float32 [1024, 1024], P(('items', 'seq'))
- grad_key: float32 [1024, 1024], P(('items', 'seq'))
- grad_value: float32 [1024, 1024], P(('items', 'seq'))
- grad_out: float32 [1024, 1024], P(('items', 'seq'))
- grad_up: float32 [1024, 4096], P(('items', 'seq'))
- grad_down: float32 [4096, 1024], P(('items', 'seq'))
- grad_ada_one: float32 [1024, 2048], P(('items', 'seq'))
- grad_ada_two: float32 [1024, 2048], P(('items', 'seq'))
- grad_table: float32 [8, 1024], P(None, ('items', 'seq'))
Inputs may be any that keep to these rules, and one draw needn't show every extreme that they name: `prompt_len`: prompt frames at and past an item's length are padding. `section_ids`: the number of items per section is uneven across sections.
All inputs are finite; a program needn't handle non-finite values.
Results may differ from a plain program's by a relative error of at most 0.019.
Values may be sent and summed in bfloat16 or wider, within the bound.
No kernel may reach another device: no remote copies, remote signals or barrier semaphores. Data moves between devices by JAX's collectives and lax.ppermute only.
A program may use at most 384 MiB of HBM per device.

v0:
```python
from functools import partial
import math
import jax
import jax.numpy as jnp
from jax import lax
from jax.sharding import PartitionSpec as P

HEADS = 16
HEAD_DIM = 64
PROMPT = 640
EPSILON = 1e-05
MASKED = -1e30


def exact(left, right):
    return jnp.dot(left, right, precision=lax.Precision.HIGHEST)


def dot_rows(left, right):
    return lax.dot_general(
        left, right, (((0,), (0,)), ((), ())), preferred_element_type=jnp.float32
    )


def dot_last(left, right):
    return lax.dot_general(
        left, right, (((1,), (1,)), ((), ())), preferred_element_type=jnp.float32
    )


def ada_norm(values, ada):
    width = values.shape[-1]
    centred = values - jnp.mean(values, axis=-1, keepdims=True)
    spread = jnp.mean(centred * centred, axis=-1, keepdims=True)
    normed = centred * lax.rsqrt(spread + EPSILON)
    return (1.0 + ada[:, None, :width]) * normed + ada[:, None, width:]


def split_heads(block):
    return block.reshape(block.shape[0], HEADS, HEAD_DIM)


def frames_major(grad, dim, items_count, seq_count):
    shape = grad.shape
    piece = shape[dim] // (items_count * seq_count)
    parted = grad.reshape(shape[:dim] + (items_count, seq_count, piece) + shape[dim + 1 :])
    return jnp.swapaxes(parted, dim, dim + 1).reshape(shape)


def shards(
    tokens,
    cotangent,
    prompt_len,
    section_ids,
    section_table,
    w_query,
    w_key,
    w_value,
    w_out,
    w_up,
    w_down,
    w_ada_one,
    w_ada_two,
):
    full_query, full_key, full_value, full_out, full_up, full_down, full_ada_one, full_ada_two = (
        lax.all_gather(w_query, "items", axis=0, tiled=True),
        lax.all_gather(w_key, "items", axis=0, tiled=True),
        lax.all_gather(w_value, "items", axis=0, tiled=True),
        lax.all_gather(w_out, "items", axis=0, tiled=True),
        lax.all_gather(w_up, "items", axis=0, tiled=True),
        lax.all_gather(w_down, "items", axis=0, tiled=True),
        lax.all_gather(w_ada_one, "items", axis=0, tiled=True),
        lax.all_gather(w_ada_two, "items", axis=0, tiled=True),
    )
    batch, rows, width = tokens.shape
    items_count = lax.axis_size("items")
    seq_count = lax.axis_size("seq")
    frames_all = rows * seq_count
    scale = 1.0 / math.sqrt(HEAD_DIM)
    position = lax.axis_index("seq") * rows + jnp.arange(rows)
    key_place = jnp.arange(frames_all)
    inputs = tokens.astype(jnp.float32)
    choose = (section_ids[:, None] == jnp.arange(section_table.shape[0])[None, :]).astype(
        jnp.float32
    )
    cond = exact(choose, section_table.astype(jnp.float32))
    ada_one_w = full_ada_one.astype(jnp.float32)
    ada_two_w = full_ada_two.astype(jnp.float32)
    ada_one = exact(cond, ada_one_w)
    ada_two = exact(cond, ada_two_w)
    normed_one, back_one = jax.vjp(ada_norm, inputs, ada_one)
    low_one = normed_one.astype(jnp.bfloat16).reshape(-1, width)
    query = (
        jnp.dot(low_one, full_query, preferred_element_type=jnp.float32)
        .astype(jnp.bfloat16)
        .reshape(batch, rows, width)
    )
    keys_here = (
        jnp.dot(low_one, full_key, preferred_element_type=jnp.float32)
        .astype(jnp.bfloat16)
        .reshape(batch, rows, width)
    )
    values_here = (
        jnp.dot(low_one, full_value, preferred_element_type=jnp.float32)
        .astype(jnp.bfloat16)
        .reshape(batch, rows, width)
    )
    keys_all, values_all = (
        lax.all_gather(keys_here, "seq", axis=1, tiled=True),
        lax.all_gather(values_here, "seq", axis=1, tiled=True),
    )

    def masked_scores(query_item, keys_item, length, query_place, key_spot):
        raw = (
            jnp.einsum(
                "qhd,khd->hqk",
                split_heads(query_item),
                split_heads(keys_item),
                preferred_element_type=jnp.float32,
            )
            * scale
        )
        allowed = (key_spot[None, :] < length) | (key_spot[None, :] >= PROMPT) & (
            query_place[:, None] >= PROMPT
        )
        return jnp.where(allowed[None], raw, MASKED)

    def attend(packed):
        query_item, keys_item, values_item, length = packed
        scores = masked_scores(query_item, keys_item, length, position, key_place)
        peak = jnp.max(scores, axis=-1, keepdims=True)
        expo = jnp.exp(scores - peak)
        total = jnp.sum(expo, axis=-1, keepdims=True)
        probs = (expo / total).astype(jnp.bfloat16)
        mixed_item = jnp.einsum(
            "hqk,khd->qhd", probs, split_heads(values_item), preferred_element_type=jnp.float32
        )
        return (
            mixed_item.astype(jnp.bfloat16).reshape(rows, width),
            (peak + jnp.log(total))[..., 0],
        )

    mixed, log_total = lax.map(attend, (query, keys_all, values_all, prompt_len))
    mixed_flat = mixed.reshape(-1, width)
    attended = inputs + jnp.dot(mixed_flat, full_out, preferred_element_type=jnp.float32).reshape(
        batch, rows, width
    )
    normed_two, back_two = jax.vjp(ada_norm, attended, ada_two)
    low_two = normed_two.astype(jnp.bfloat16).reshape(-1, width)
    upward = jnp.dot(low_two, full_up, preferred_element_type=jnp.float32)
    active, gelu_back = jax.vjp(partial(jax.nn.gelu, approximate=False), upward)
    active_low = active.astype(jnp.bfloat16)
    layer_out = (
        attended
        + jnp.dot(active_low, full_down, preferred_element_type=jnp.float32).reshape(
            batch, rows, width
        )
    ).astype(jnp.bfloat16)
    grad_top = cotangent.astype(jnp.float32)
    grad_low = cotangent.reshape(-1, width)
    grad_down = dot_rows(active_low, grad_low)
    (grad_upward,) = gelu_back(dot_last(grad_low, full_down))
    upward_low = grad_upward.astype(jnp.bfloat16)
    grad_up = dot_rows(low_two, upward_low)
    grad_normed_two = dot_last(upward_low, full_up).reshape(batch, rows, width)
    back_mid, grad_ada_two_rows = back_two(grad_normed_two)
    grad_attended = grad_top + back_mid
    grad_ada_two = exact(cond.T, grad_ada_two_rows)
    attended_low = grad_attended.astype(jnp.bfloat16).reshape(-1, width)
    grad_out = dot_rows(mixed_flat, attended_low)
    grad_mixed = dot_last(attended_low, full_out).astype(jnp.bfloat16).reshape(batch, rows, width)

    def score_grads(
        query_item, keys_item, values_item, length, log_item, grad_item, query_place, key_spot
    ):
        scores = masked_scores(query_item, keys_item, length, query_place, key_spot)
        probs = jnp.exp(scores - log_item[..., None])
        grad_heads = split_heads(grad_item)
        grad_probs = jnp.einsum(
            "qhd,khd->hqk", grad_heads, split_heads(values_item), preferred_element_type=jnp.float32
        )
        inner = jnp.sum(probs * grad_probs, axis=-1, keepdims=True)
        grad_scores = (probs * (grad_probs - inner)).astype(jnp.bfloat16)
        return (probs, grad_heads, grad_scores, inner[..., 0])

    def attend_back(packed):
        query_item, keys_item, values_item, length, log_item, grad_item = packed
        probs, grad_heads, grad_scores, inner = score_grads(
            query_item, keys_item, values_item, length, log_item, grad_item, position, key_place
        )
        grad_query_item = (
            jnp.einsum(
                "hqk,khd->qhd",
                grad_scores,
                split_heads(keys_item),
                preferred_element_type=jnp.float32,
            )
            * scale
        )
        grad_keys_item = (
            jnp.einsum(
                "hqk,qhd->khd",
                grad_scores,
                split_heads(query_item),
                preferred_element_type=jnp.float32,
            )
            * scale
        )
        grad_values_item = jnp.einsum(
            "hqk,qhd->khd",
            probs.astype(jnp.bfloat16),
            grad_heads,
            preferred_element_type=jnp.float32,
        )
        return (
            grad_query_item.reshape(rows, width),
            grad_keys_item.reshape(frames_all, width),
            grad_values_item.reshape(frames_all, width),
        )

    grad_query_rows, grad_keys_all, grad_values_all = lax.map(
        attend_back, (query, keys_all, values_all, prompt_len, log_total, grad_mixed)
    )
    grad_keys_here, grad_values_here = (
        lax.psum_scatter(
            grad_keys_all.astype(jnp.bfloat16), "seq", scatter_dimension=1, tiled=True
        ).astype(jnp.float32),
        lax.psum_scatter(
            grad_values_all.astype(jnp.bfloat16), "seq", scatter_dimension=1, tiled=True
        ).astype(jnp.float32),
    )
    query_low = grad_query_rows.astype(jnp.bfloat16).reshape(-1, width)
    keys_low = grad_keys_here.astype(jnp.bfloat16).reshape(-1, width)
    values_low = grad_values_here.astype(jnp.bfloat16).reshape(-1, width)
    grad_query = dot_rows(low_one, query_low)
    grad_key = dot_rows(low_one, keys_low)
    grad_value = dot_rows(low_one, values_low)
    grad_normed_one = (
        dot_last(query_low, full_query)
        + dot_last(keys_low, full_key)
        + dot_last(values_low, full_value)
    )
    back_in, grad_ada_one_rows = back_one(grad_normed_one.reshape(batch, rows, width))
    input_grad = grad_attended + back_in
    grad_ada_one = exact(cond.T, grad_ada_one_rows)
    grad_cond = exact(grad_ada_one_rows, ada_one_w.T) + exact(grad_ada_two_rows, ada_two_w.T)
    grad_table = exact(choose.T, grad_cond)
    table_t = frames_major(grad_table, 1, items_count, seq_count)
    part_query = frames_major(grad_query, 0, items_count, seq_count)
    part_key = frames_major(grad_key, 0, items_count, seq_count)
    part_value = frames_major(grad_value, 0, items_count, seq_count)
    part_out = frames_major(grad_out, 0, items_count, seq_count)
    part_ada_one = frames_major(grad_ada_one, 0, items_count, seq_count)
    part_up = frames_major(grad_up, 0, items_count, seq_count)
    part_down = frames_major(grad_down, 0, items_count, seq_count)
    part_ada_two = frames_major(grad_ada_two, 0, items_count, seq_count)
    (
        seq_query,
        seq_key,
        seq_value,
        seq_out,
        seq_up,
        seq_down,
        seq_ada_one,
        seq_ada_two,
        seq_table,
    ) = (
        lax.psum_scatter(
            part_query.astype(jnp.bfloat16), "seq", scatter_dimension=0, tiled=True
        ).astype(jnp.float32),
        lax.psum_scatter(
            part_key.astype(jnp.bfloat16), "seq", scatter_dimension=0, tiled=True
        ).astype(jnp.float32),
        lax.psum_scatter(
            part_value.astype(jnp.bfloat16), "seq", scatter_dimension=0, tiled=True
        ).astype(jnp.float32),
        lax.psum_scatter(
            part_out.astype(jnp.bfloat16), "seq", scatter_dimension=0, tiled=True
        ).astype(jnp.float32),
        lax.psum_scatter(
            part_up.astype(jnp.bfloat16), "seq", scatter_dimension=0, tiled=True
        ).astype(jnp.float32),
        lax.psum_scatter(
            part_down.astype(jnp.bfloat16), "seq", scatter_dimension=0, tiled=True
        ).astype(jnp.float32),
        lax.psum_scatter(
            part_ada_one.astype(jnp.bfloat16), "seq", scatter_dimension=0, tiled=True
        ).astype(jnp.float32),
        lax.psum_scatter(
            part_ada_two.astype(jnp.bfloat16), "seq", scatter_dimension=0, tiled=True
        ).astype(jnp.float32),
        lax.psum_scatter(
            table_t.astype(jnp.bfloat16), "seq", scatter_dimension=1, tiled=True
        ).astype(jnp.float32),
    )
    (
        grad_query,
        grad_key,
        grad_value,
        grad_out,
        grad_up,
        grad_down,
        grad_ada_one,
        grad_ada_two,
        grad_table,
    ) = (
        lax.psum_scatter(
            seq_query.astype(jnp.bfloat16), "items", scatter_dimension=0, tiled=True
        ).astype(jnp.float32),
        lax.psum_scatter(
            seq_key.astype(jnp.bfloat16), "items", scatter_dimension=0, tiled=True
        ).astype(jnp.float32),
        lax.psum_scatter(
            seq_value.astype(jnp.bfloat16), "items", scatter_dimension=0, tiled=True
        ).astype(jnp.float32),
        lax.psum_scatter(
            seq_out.astype(jnp.bfloat16), "items", scatter_dimension=0, tiled=True
        ).astype(jnp.float32),
        lax.psum_scatter(
            seq_up.astype(jnp.bfloat16), "items", scatter_dimension=0, tiled=True
        ).astype(jnp.float32),
        lax.psum_scatter(
            seq_down.astype(jnp.bfloat16), "items", scatter_dimension=0, tiled=True
        ).astype(jnp.float32),
        lax.psum_scatter(
            seq_ada_one.astype(jnp.bfloat16), "items", scatter_dimension=0, tiled=True
        ).astype(jnp.float32),
        lax.psum_scatter(
            seq_ada_two.astype(jnp.bfloat16), "items", scatter_dimension=0, tiled=True
        ).astype(jnp.float32),
        lax.psum_scatter(
            seq_table.astype(jnp.bfloat16), "items", scatter_dimension=1, tiled=True
        ).astype(jnp.float32),
    )
    return (
        layer_out,
        input_grad,
        grad_query,
        grad_key,
        grad_value,
        grad_out,
        grad_up,
        grad_down,
        grad_ada_one,
        grad_ada_two,
        grad_table,
    )


def solution(mesh):
    return jax.shard_map(
        shards,
        mesh=mesh,
        in_specs=(
            P("items", "seq", None),
            P("items", "seq", None),
            P("items"),
            P("items"),
            P(),
            P("items", None),
            P("items", None),
            P("items", None),
            P("items", None),
            P("items", None),
            P("items", None),
            P("items", None),
            P("items", None),
        ),
        out_specs=(
            P("items", "seq", None),
            P("items", "seq", None),
            P(("items", "seq"), None),
            P(("items", "seq"), None),
            P(("items", "seq"), None),
            P(("items", "seq"), None),
            P(("items", "seq"), None),
            P(("items", "seq"), None),
            P(("items", "seq"), None),
            P(("items", "seq"), None),
            P(None, ("items", "seq")),
        ),
        check_vma=False,
    )
```

profile of v0, /device:TPU:0, one launch (start us, length us, event | category | flops | bytes accessed | tf_op | source)
XLA Modules:
  0.0 1794.8 jit_solution(3981334618277993144)
XLA Ops:
  14.1 49.4 %all-gather.13.cloned.1.call-done = bf16[1024,2048]{1,0:T(8,128)(2,1)} async-done(((bf16[64,2048]{1,0:T(8,128)(2,1)}), bf16[1024,2048]{1,0:T(8,128)(2,1)}) %all-gather.13.cloned.1.call-update) | async-done | bytes 4194320 | tf_op jit(solution)/shard_map/all_gather | solution.py:72
  63.5 3.9 fusion.75
  67.4 38.1 %all-gather.19.cloned.1.call-done = bf16[1024,1024]{1,0:T(8,128)(2,1)} async-done(((bf16[64,1024]{1,0:T(8,128)(2,1)}), bf16[1024,1024]{1,0:T(8,128)(2,1)}) %all-gather.19.cloned.1.call-update) | async-done | bytes 2097168 | tf_op jit(solution)/shard_map/all_gather | solution.py:67
  105.6 4.2 convolution_convert_fusion.1
  109.9 38.1 %all-gather.15.cloned.1.call-done = bf16[1024,1024]{1,0:T(8,128)(2,1)} async-done(((bf16[64,1024]{1,0:T(8,128)(2,1)}), bf16[1024,1024]{1,0:T(8,128)(2,1)}) %all-gather.15.cloned.1.call-update) | async-done | bytes 2097168 | tf_op jit(solution)/shard_map/all_gather | solution.py:68
  148.0 4.2 convolution_convert_fusion.3
  155.7 43.8 %all-gather.23.cloned.1.call-done = bf16[1024,2048]{1,0:T(8,128)(2,1)} async-done(((bf16[64,2048]{1,0:T(8,128)(2,1)}), bf16[1024,2048]{1,0:T(8,128)(2,1)}) %all-gather.23.cloned.1.call-update) | async-done | bytes 4194320 | tf_op jit(solution)/shard_map/all_gather | solution.py:73
  199.5 3.9 fusion.73
  203.4 38.0 %all-gather.17.cloned.1.call-done = bf16[1024,1024]{1,0:T(8,128)(2,1)} async-done(((bf16[64,1024]{1,0:T(8,128)(2,1)}), bf16[1024,1024]{1,0:T(8,128)(2,1)}) %all-gather.17.cloned.1.call-update) | async-done | bytes 2097168 | tf_op jit(solution)/shard_map/all_gather | solution.py:66
  241.5 3.2 convolution_convert_fusion.2
  246.1 35.2 %all-gather.31.cloned.1.call-done = bf16[1280,1024]{1,0:T(8,128)(2,1)} async-done(((bf16[640,1024]{1,0:T(8,128)(2,1)}), bf16[1280,1024]{1,0:T(8,128)(2,1)}) %all-gather.31.cloned.1.call-update) | async-done | bytes 2621456 | tf_op jit(solution)/shard_map/all_gather | solution.py:109
  281.3 3.0 copy.60
  284.3 23.1 %fusion.93 = (f32[16,640]{1,0:T(8,128)S(1)}, f32[16,640,1280]{2,1,0:T(8,128)}) fusion(bf16[640,16,64]{0,2,1:T(8,128)(2,1)} %bitcast.284, bf16[1280,16,64]{0,2,1:T(8,128)(2,1)S(1)} %bitcast.278, pred[640,1280]{1,0:T(8,128)(4,1)S(1)} %and_or_fusion), kind=kOutput, calls=%fused_computation.153 | convolution fusion | flops 1717032960 | bytes 57221120 | tf_op jit(solution)/shard_map/while/body/eval_jaxpr/qhd,khd->hqk/dot_general | solution.py:115
  307.4 16.8 fusion
  324.2 4.4 copy.58
  328.6 20.2 %fusion.50 = bf16[16,64,640]{2,1,0:T(8,128)(2,1)S(1)} fusion(bf16[1280,16,64]{0,2,1:T(8,128)(2,1)} %bitcast.289, f32[16,640,1280]{2,1,0:T(8,128)} %get-tuple-element.90, f32[16,640]{1,0:T(8,128)S(1)} %fusion, f32[16,640]{1,0:T(8,128)S(1)} %get-tuple-element.89), kind=kOutput, calls=%fused_computation.97 | convolution fusion | flops 1717698560 | bytes 56442880 | tf_op jit(solution)/shard_map/while/body/eval_jaxpr/hqk,khd->qhd/dot_general | solution.py:135
  348.8 17.3 all-gather.21.cloned.1.call-done
  366.1 3.2 fusion.94
  371.3 70.7 %all-gather.25.cloned.1.call-done = bf16[1024,4096]{1,0:T(8,128)(2,1)} async-done(((bf16[64,4096]{1,0:T(8,128)(2,1)}), bf16[1024,4096]{1,0:T(8,128)(2,1)}) %all-gather.25.cloned.1.call-update) | async-done | bytes 8388624 | tf_op jit(solution)/shard_map/all_gather | solution.py:70
  442.0 32.4 %fusion.6 = (f32[640,4096]{1,0:T(8,128)}, f32[640,4096]{1,0:T(8,128)}) fusion(bf16[1024,4096]{1,0:T(8,128)(2,1)} %all-gather.25.cloned.1.call-done, f32[1024]{0:T(1024)S(1)} %bitcast.330, f32[640]{0:T(1024)S(1)} %fusion.78, f32[1,640,1024]{2,1,0:T(8,128)} %copy-done.6, f32[640]{0:T(1024)S(1)} %broadcast_multiply_fusion, f32[1024]{0:T(1024)S(1)} %bitcast.310), kind=kOutput, calls=%fused_computation.13 | convolution fusion | flops 5534515200 | bytes 31994880 | tf_op jit(solution)/shard_map/dot_general | solution.py:150
  474.4 42.8 %all-gather.27.cloned.1.call-done = bf16[4096,1024]{1,0:T(8,128)(2,1)} async-done(((bf16[256,1024]{1,0:T(8,128)(2,1)}), bf16[4096,1024]{1,0:T(8,128)(2,1)}) %all-gather.27.cloned.1.call-update) | async-done | bytes 8388624 | tf_op jit(solution)/shard_map/all_gather | solution.py:71
  517.2 16.8 add_convert_fusion
  533.9 10.2 fusion.95
  544.2 2.1 fusion.46
  552.4 38.6 %multiply_reduce_fusion = (f32[16,640]{1,0:T(8,128)S(1)}, f32[16,640,1280]{2,1,0:T(8,128)}) fusion(f32[16,640,1280]{2,1,0:T(8,128)} %get-tuple-element.90, f32[16,640]{1,0:T(8,128)S(1)} %log_add_fusion, bf16[640,16,64]{0,2,1:T(8,128)(2,1)S(1)} %bitcast.287, bf16[1280,16,64]{0,2,1:T(8,128)(2,1)} %bitcast.290), kind=kOutput, calls=%fused_computation.1 | convolution fusion | flops 1717032960 | bytes 108871680 | tf_op jit(solution)/shard_map/while/body/eval_jaxpr/qhd,khd->hqk/dot_general | solution.py:179
  591.0 42.2 %multiply_convert_fusion = bf16[16,640,1280]{2,1,0:T(8,128)(2,1)} fusion(f32[16,640,1280]{2,1,0:T(8,128)} %get-tuple-element.96, f32[16,640,1280]{2,1,0:T(8,128)} %get-tuple-element.90, f32[16,640]{1,0:T(8,128)S(1)} %get-tuple-element.95, f32[16,640]{1,0:T(8,128)S(1)} %log_add_fusion), kind=kLoop, calls=%fused_computation | loop fusion | flops 52428800 | bytes 131153920 | tf_op jit(solution)/shard_map/while/body/eval_jaxpr/convert_element_type | solution.py:183
  633.2 14.6 multiply_convert_fusion.5
  647.8 4.5 copy.62
  652.4 21.5 %fusion.36 = bf16[16,64,1280]{2,1,0:T(8,128)(2,1)} fusion(bf16[640,16,64]{0,2,1:T(8,128)(2,1)S(1)} %bitcast.288, f32[16,640,1280]{2,1,0:T(8,128)} %get-tuple-element.90, f32[16,640]{1,0:T(8,128)S(1)} %log_add_fusion), kind=kOutput, calls=%fused_computation.67 | convolution fusion | flops 1705246720 | bytes 56401920 | tf_op jit(solution)/shard_map/while/body/eval_jaxpr/hqk,qhd->khd/dot_general | solution.py:209
  673.9 4.5 copy.63
  678.5 5.7 fusion.69
  684.2 14.9 multiply_convert_fusion.6
  699.0 5.2 fusion.96
  704.2 4.4 fusion.56
  708.7 19.5 %reduce-scatter.25.cloned.1.call-done = bf16[1,640,1024]{2,1,0:T(8,128)(2,1)} async-done(((bf16[1,1280,1024]{2,1,0:T(8,128)(2,1)}), bf16[1,640,1024]{2,1,0:T(8,128)(2,1)}) %reduce-scatter.25.cloned.1.call-update) | async-done | bytes 1310736 | tf_op jit(solution)/shard_map/reduce_scatter | solution.py:228
  728.2 5.9 fusion.45
  734.7 2.5 fusion.43
  737.2 5.5 fusion.71
  744.1 3.5 convert_bitcast_fusion.2
  749.3 4.5 fusion.90
  759.3 1.8 convert_bitcast_fusion.5
  766.8 6.4 multiply_convert_fusion.2
  775.4 11.5 convert_bitcast_fusion.1
  786.9 7.8 copy.71
  794.7 24.6 %fusion.9 = bf16[4096,640]{0,1:T(8,128)(2,1)} fusion(f32[640,4096]{1,0:T(8,128)} %get-tuple-element.94), kind=kLoop, calls=%fused_computation.16 | loop fusion | flops 170393600 | bytes 15728640 | tf_op jit(solution)/shard_map/convert_element_type | solution.py:152
  819.4 7.9 copy.83
  827.3 11.6 convert_bitcast_fusion
  838.9 8.2 copy.73
  850.1 5.5 reduce-scatter.27.cloned.1.call-done
  855.6 34.0 %reduce-scatter.31.cloned.1.call-done = bf16[512,1024]{1,0:T(8,128)(2,1)} async-done(((bf16[1024,1024]{1,0:T(8,128)(2,1)}), bf16[512,1024]{1,0:T(8,128)(2,1)}) %reduce-scatter.31.cloned.1.call-update) | async-done | bytes 1048592 | tf_op jit(solution)/shard_map/reduce_scatter | solution.py:271
  889.7 56.4 %reduce-scatter.55.cloned.1.call-done = bf16[512,2048]{1,0:T(8,128)(2,1)} async-done(((bf16[1024,2048]{1,0:T(8,128)(2,1)}), bf16[512,2048]{1,0:T(8,128)(2,1)}) %reduce-scatter.55.cloned.1.call-update) | async-done | bytes 2097168 | tf_op jit(solution)/shard_map/reduce_scatter | solution.py:289
  946.2 56.7 %reduce-scatter.51.cloned.1.call-done = bf16[512,2048]{1,0:T(8,128)(2,1)} async-done(((bf16[1024,2048]{1,0:T(8,128)(2,1)}), bf16[512,2048]{1,0:T(8,128)(2,1)}) %reduce-scatter.51.cloned.1.call-update) | async-done | bytes 2097168 | tf_op jit(solution)/shard_map/reduce_scatter | solution.py:286
  1002.9 101.3 %reduce-scatter.43.cloned.1.call-done = bf16[512,4096]{1,0:T(8,128)(2,1)} async-done(((bf16[1024,4096]{1,0:T(8,128)(2,1)}), bf16[512,4096]{1,0:T(8,128)(2,1)}) %reduce-scatter.43.cloned.1.call-update) | async-done | bytes 4194320 | tf_op jit(solution)/shard_map/reduce_scatter | solution.py:280
  1104.5 101.4 %reduce-scatter.47.cloned.1.call-done = bf16[2048,1024]{1,0:T(8,128)(2,1)} async-done(((bf16[4096,1024]{1,0:T(8,128)(2,1)}), bf16[2048,1024]{1,0:T(8,128)(2,1)}) %reduce-scatter.47.cloned.1.call-update) | async-done | bytes 4194320 | tf_op jit(solution)/shard_map/reduce_scatter | solution.py:283
  1206.0 13.2 fusion.48
  1219.1 45.9 %reduce-scatter.61.cloned.1.call-done = bf16[32,8]{1,0:T(8,128)(2,1)} async-done(((bf16[512,8]{1,0:T(8,128)(2,1)}), bf16[32,8]{1,0:T(8,128)(2,1)}) %reduce-scatter.61.cloned.1.call-update) | async-done | bytes 528
  1266.4 58.7 %reduce-scatter.41.cloned.1.call-done = bf16[32,1024]{1,0:T(8,128)(2,1)} async-done(((bf16[512,1024]{1,0:T(8,128)(2,1)}), bf16[32,1024]{1,0:T(8,128)(2,1)}) %reduce-scatter.41.cloned.1.call-update) | async-done | bytes 65552 | tf_op jit(solution)/shard_map/reduce_scatter | solution.py:316
  1326.6 58.9 %reduce-scatter.37.cloned.1.call-done = bf16[32,1024]{1,0:T(8,128)(2,1)} async-done(((bf16[512,1024]{1,0:T(8,128)(2,1)}), bf16[32,1024]{1,0:T(8,128)(2,1)}) %reduce-scatter.37.cloned.1.call-update) | async-done | bytes 65552 | tf_op jit(solution)/shard_map/reduce_scatter | solution.py:313
  1387.1 58.5 %reduce-scatter.29.cloned.1.call-done = bf16[32,1024]{1,0:T(8,128)(2,1)} async-done(((bf16[512,1024]{1,0:T(8,128)(2,1)}), bf16[32,1024]{1,0:T(8,128)(2,1)}) %reduce-scatter.29.cloned.1.call-update) | async-done | bytes 65552 | tf_op jit(solution)/shard_map/reduce_scatter | solution.py:307
  1447.0 58.9 %reduce-scatter.33.cloned.1.call-done = bf16[32,1024]{1,0:T(8,128)(2,1)} async-done(((bf16[512,1024]{1,0:T(8,128)(2,1)}), bf16[32,1024]{1,0:T(8,128)(2,1)}) %reduce-scatter.33.cloned.1.call-update) | async-done | bytes 65552 | tf_op jit(solution)/shard_map/reduce_scatter | solution.py:310
  1507.4 62.7 %reduce-scatter.57.cloned.1.call-done = bf16[32,2048]{1,0:T(8,128)(2,1)} async-done(((bf16[512,2048]{1,0:T(8,128)(2,1)}), bf16[32,2048]{1,0:T(8,128)(2,1)}) %reduce-scatter.57.cloned.1.call-update) | async-done | bytes 131088 | tf_op jit(solution)/shard_map/reduce_scatter | solution.py:328
  1571.8 63.1 %reduce-scatter.53.cloned.1.call-done = bf16[32,2048]{1,0:T(8,128)(2,1)} async-done(((bf16[512,2048]{1,0:T(8,128)(2,1)}), bf16[32,2048]{1,0:T(8,128)(2,1)}) %reduce-scatter.53.cloned.1.call-update) | async-done | bytes 131088 | tf_op jit(solution)/shard_map/reduce_scatter | solution.py:325
  1636.5 73.8 %reduce-scatter.45.cloned.1.call-done = bf16[32,4096]{1,0:T(8,128)(2,1)} async-done(((bf16[512,4096]{1,0:T(8,128)(2,1)}), bf16[32,4096]{1,0:T(8,128)(2,1)}) %reduce-scatter.45.cloned.1.call-update) | async-done | bytes 262160 | tf_op jit(solution)/shard_map/reduce_scatter | solution.py:319
  1712.1 73.8 %reduce-scatter.49.cloned.1.call-done = bf16[128,1024]{1,0:T(8,128)(2,1)} async-done(((bf16[2048,1024]{1,0:T(8,128)(2,1)}), bf16[128,1024]{1,0:T(8,128)(2,1)}) %reduce-scatter.49.cloned.1.call-update) | async-done | bytes 262160 | tf_op jit(solution)/shard_map/reduce_scatter | solution.py:322
  (184 shorter events, 52.9 us)
Async XLA Ops:
  7.2 6.8 copy-start
  7.2 5.7 copy-start.4
  7.2 56.3 %all-gather.13.cloned.1.call-start = ((), (), s32[]{:S(2)}) async-start(), calls=%async_computation.20 | async-start | bytes 4456448 | tf_op jit(solution)/shard_map/all_gather | solution.py:72
  7.9 97.6 %all-gather.19.cloned.1.call-start = ((), (), s32[]{:S(2)}) async-start(), calls=%async_computation.23 | async-start | bytes 2228224 | tf_op jit(solution)/shard_map/all_gather | solution.py:67
  8.7 139.3 %all-gather.15.cloned.1.call-start = ((), (), s32[]{:S(2)}) async-start(), calls=%async_computation.21 | async-start | bytes 2228224 | tf_op jit(solution)/shard_map/all_gather | solution.py:68
  9.4 190.1 %all-gather.23.cloned.1.call-start = ((), (), s32[]{:S(2)}) async-start(), calls=%async_computation.25 | async-start | bytes 4456448 | tf_op jit(solution)/shard_map/all_gather | solution.py:73
  10.0 231.5 %all-gather.17.cloned.1.call-start = ((), (), s32[]{:S(2)}) async-start(), calls=%async_computation.22 | async-start | bytes 2228224 | tf_op jit(solution)/shard_map/all_gather | solution.py:66
  10.6 270.7 %all-gather.31.cloned.1.call-start = ((), (), s32[]{:S(2)}) async-start(), calls=%async_computation.48 | async-start | bytes 3932160 | tf_op jit(solution)/shard_map/all_gather | solution.py:109
  12.9 228.6 %copy-start.17 = (f32[640]{0:T(1024)}, f32[640]{0:T(1024)S(1)}, u32[]{:S(2)}) copy-start(f32[640]{0:T(1024)S(1)} %broadcast_multiply_fusion.1) | copy-start | bytes 7684
  13.3 0.6 copy-start.25
  13.9 227.5 %copy-start.21 = (f32[640]{0:T(1024)}, f32[640]{0:T(1024)S(1)}, u32[]{:S(2)}) copy-start(f32[640]{0:T(1024)S(1)} %fusion.77) | copy-start | bytes 7684
  14.1 185.4 %copy-start.23 = (f32[1,1024]{1,0:T(1,128)}, f32[1,1024]{1,0:T(1,128)S(1)}, u32[]{:S(2)}) copy-start(f32[1,1024]{1,0:T(1,128)S(1)} %fusion.79) | copy-start | bytes 12292
  67.4 174.1 %copy-start.19 = (f32[1,1024]{1,0:T(1,128)}, f32[1,1024]{1,0:T(1,128)S(1)}, u32[]{:S(2)}) copy-start(f32[1,1024]{1,0:T(1,128)S(1)} %get-tuple-element.87) | copy-start | bytes 12292
  67.4 174.0 %copy-start.27 = (f32[1,1024]{1,0:T(1,128)}, f32[1,1024]{1,0:T(1,128)S(1)}, u32[]{:S(2)}) copy-start(f32[1,1024]{1,0:T(1,128)S(1)} %get-tuple-element.88) | copy-start | bytes 12292
  109.8 214.4 %all-gather.29.cloned.1.call-start = ((), (), s32[]{:S(2)}) async-start(), calls=%async_computation.47 | async-start | bytes 3932160 | tf_op jit(solution)/shard_map/all_gather | solution.py:110
  152.2 213.9 %all-gather.21.cloned.1.call-start = ((), (), s32[]{:S(2)}) async-start(), calls=%async_computation.24 | async-start | bytes 2228224 | tf_op jit(solution)/shard_map/all_gather | solution.py:69
  153.0 289.0 %all-gather.25.cloned.1.call-start = ((), (), s32[]{:S(2)}) async-start(), calls=%async_computation.26 | async-start | bytes 8912896 | tf_op jit(solution)/shard_map/all_gather | solution.py:70
  153.7 363.5 %all-gather.27.cloned.1.call-start = ((), (), s32[]{:S(2)}) async-start(), calls=%async_computation.27 | async-start | bytes 8912896 | tf_op jit(solution)/shard_map/all_gather | solution.py:71
  154.3 550.0 %reduce-scatter.23.cloned.1.call-start = ((), (), s32[]{:S(2)}) async-start(), calls=%async_computation.28 | async-start | bytes 3932160 | tf_op jit(solution)/shard_map/reduce_scatter | solution.py:225
  284.2 23.1 %copy-start.2 = (bf16[1280,1024]{0,1:T(8,128)(2,1)}, bf16[1280,1024]{0,1:T(8,128)(2,1)S(1)}, u32[]{:S(2)}) copy-start(bf16[1280,1024]{0,1:T(8,128)(2,1)S(1)} %copy.60) | copy-start | bytes 7864324
  328.6 37.5 %copy-start.5 = (bf16[1,640,1024]{2,1,0:T(8,128)(2,1)S(1)}, bf16[1,640,1024]{2,1,0:T(8,128)(2,1)}, u32[]{:S(2)}) copy-start(bf16[1,640,1024]{2,1,0:T(8,128)(2,1)} %param.13) | copy-start | bytes 3932164
  348.8 20.6 %copy-start.32 = (bf16[16,64,640]{2,1,0:T(8,128)(2,1)}, bf16[16,64,640]{2,1,0:T(8,128)(2,1)S(1)}, u32[]{:S(2)}) copy-start(bf16[16,64,640]{2,1,0:T(8,128)(2,1)S(1)} %fusion.50) | copy-start | bytes 3932164
  369.3 1.5 copy-start.6
  442.0 75.2 %copy-start.12 = (bf16[1,640,1024]{2,1,0:T(8,128)(2,1)S(1)}, bf16[1,640,1024]{2,1,0:T(8,128)(2,1)}, u32[]{:S(2)}) copy-start(bf16[1,640,1024]{2,1,0:T(8,128)(2,1)} %param.14) | copy-start | bytes 3932164
  533.9 10.3 copy-start.7
  547.2 1.5 copy-start.9
  547.2 2.8 copy-start.30
  548.6 1.0 copy-start.16
  591.0 42.2 %copy-start.10 = (bf16[640,1024]{0,1:T(8,128)(2,1)S(1)}, bf16[640,1024]{0,1:T(8,128)(2,1)}, u32[]{:S(2)}) copy-start(bf16[640,1024]{0,1:T(8,128)(2,1)} %copy.59) | copy-start | bytes 3932164
  652.4 75.8 %reduce-scatter.25.cloned.1.call-start = ((), (), s32[]{:S(2)}) async-start(), calls=%async_computation.29 | async-start | bytes 3932160 | tf_op jit(solution)/shard_map/reduce_scatter | solution.py:228
  678.4 5.8 copy-start.3
  678.4 168.8 %reduce-scatter.59.cloned.1.call-start = ((), (), s32[]{:S(2)}) async-start(), calls=%async_computation.46 | async-start | bytes 24576 | tf_op jit(solution)/shard_map/reduce_scatter | solution.py:292
  699.0 5.2 copy-start.29
  704.2 23.9 %copy-start.18 = (f32[640]{0:T(1024)S(1)}, f32[640]{0:T(1024)}, u32[]{:S(2)}) copy-start(f32[640]{0:T(1024)} %copy-done.17) | copy-start | bytes 7684
  704.2 23.9 %copy-start.20 = (f32[1,1024]{1,0:T(1,128)S(1)}, f32[1,1024]{1,0:T(1,128)}, u32[]{:S(2)}) copy-start(f32[1,1024]{1,0:T(1,128)} %copy-done.19) | copy-start | bytes 12292
  708.7 25.4 %copy-start.26 = (f32[640]{0:T(1024)S(1)}, f32[640]{0:T(1024)}, u32[]{:S(2)}) copy-start(f32[640]{0:T(1024)} %copy-done.25) | copy-start | bytes 7684
  734.0 0.7 copy-start.22
  743.7 105.1 %reduce-scatter.39.cloned.1.call-start = ((), (), s32[]{:S(2)}) async-start(), calls=%async_computation.36 | async-start | bytes 3145728 | tf_op jit(solution)/shard_map/reduce_scatter | solution.py:277
  747.6 1.6 copy-start.28
  749.2 100.3 %reduce-scatter.35.cloned.1.call-start = ((), (), s32[]{:S(2)}) async-start(), calls=%async_computation.34 | async-start | bytes 3145728 | tf_op jit(solution)/shard_map/reduce_scatter | solution.py:274
  753.8 1.8 copy-start.15
  757.4 1.8 copy-start.14
  758.9 96.6 %reduce-scatter.27.cloned.1.call-start = ((), (), s32[]{:S(2)}) async-start(), calls=%async_computation.30 | async-start | bytes 3145728 | tf_op jit(solution)/shard_map/reduce_scatter | solution.py:268
  761.1 2.2 copy-start.31
  762.6 127.0 %reduce-scatter.31.cloned.1.call-start = ((), (), s32[]{:S(2)}) async-start(), calls=%async_computation.32 | async-start | bytes 3145728 | tf_op jit(solution)/shard_map/reduce_scatter | solution.py:271
  765.1 1.6 copy-start.24
  766.7 179.4 %reduce-scatter.55.cloned.1.call-start = ((), (), s32[]{:S(2)}) async-start(), calls=%async_computation.44 | async-start | bytes 6291456 | tf_op jit(solution)/shard_map/reduce_scatter | solution.py:289
  773.3 1.3 copy-start.11
  773.3 229.5 %reduce-scatter.51.cloned.1.call-start = ((), (), s32[]{:S(2)}) async-start(), calls=%async_computation.42 | async-start | bytes 6291456 | tf_op jit(solution)/shard_map/reduce_scatter | solution.py:286
  774.1 330.2 %reduce-scatter.43.cloned.1.call-start = ((), (), s32[]{:S(2)}) async-start(), calls=%async_computation.38 | async-start | bytes 12582912 | tf_op jit(solution)/shard_map/reduce_scatter | solution.py:280
  794.7 411.2 %reduce-scatter.47.cloned.1.call-start = ((), (), s32[]{:S(2)}) async-start(), calls=%async_computation.40 | async-start | bytes 12582912 | tf_op jit(solution)/shard_map/reduce_scatter | solution.py:283
  819.4 7.9 copy-start.13
  847.1 417.9 %reduce-scatter.61.cloned.1.call-start = ((), (), s32[]{:S(2)}) async-start(), calls=%async_computation.49 | async-start | bytes 139264
  848.7 476.4 %reduce-scatter.41.cloned.1.call-start = ((), (), s32[]{:S(2)}) async-start(), calls=%async_computation.37 | async-start | bytes 1114112 | tf_op jit(solution)/shard_map/reduce_scatter | solution.py:316
  849.5 536.1 %reduce-scatter.37.cloned.1.call-start = ((), (), s32[]{:S(2)}) async-start(), calls=%async_computation.35 | async-start | bytes 1114112 | tf_op jit(solution)/shard_map/reduce_scatter | solution.py:313
  850.0 595.5 %reduce-scatter.29.cloned.1.call-start = ((), (), s32[]{:S(2)}) async-start(), calls=%async_computation.31 | async-start | bytes 1114112 | tf_op jit(solution)/shard_map/reduce_scatter | solution.py:307
  855.6 650.3 %reduce-scatter.33.cloned.1.call-start = ((), (), s32[]{:S(2)}) async-start(), calls=%async_computation.33 | async-start | bytes 1114112 | tf_op jit(solution)/shard_map/reduce_scatter | solution.py:310
  889.6 680.5 %reduce-scatter.57.cloned.1.call-start = ((), (), s32[]{:S(2)}) async-start(), calls=%async_computation.45 | async-start | bytes 2228224 | tf_op jit(solution)/shard_map/reduce_scatter | solution.py:328
  946.1 688.8 %reduce-scatter.53.cloned.1.call-start = ((), (), s32[]{:S(2)}) async-start(), calls=%async_computation.43 | async-start | bytes 2228224 | tf_op jit(solution)/shard_map/reduce_scatter | solution.py:325
  1002.9 707.5 %reduce-scatter.45.cloned.1.call-start = ((), (), s32[]{:S(2)}) async-start(), calls=%async_computation.39 | async-start | bytes 4456448 | tf_op jit(solution)/shard_map/reduce_scatter | solution.py:319
  1104.3 101.7 %copy-start.8 = (f32[1,640,1024]{2,1,0:T(8,128)S(1)}, f32[1,640,1024]{2,1,0:T(8,128)}, u32[]{:S(2)}) copy-start(f32[1,640,1024]{2,1,0:T(8,128)} %copy-done.6) | copy-start | bytes 7864324
  1104.3 681.6 %reduce-scatter.49.cloned.1.call-start = ((), (), s32[]{:S(2)}) async-start(), calls=%async_computation.41 | async-start | bytes 4456448 | tf_op jit(solution)/shard_map/reduce_scatter | solution.py:322
  1206.0 581.7 %copy-start.1 = (bf16[8,1024]{1,0:T(8,128)(2,1)S(1)}, bf16[8,1024]{1,0:T(8,128)(2,1)}, u32[]{:S(2)}) copy-start(bf16[8,1024]{1,0:T(8,128)(2,1)} %param.17) | copy-start | bytes 49156
Sparse Core Ops, SparseCore 0:
  10.2 53.2 all-gather.12
  65.7 39.8 all-gather.18
  107.7 40.1 all-gather.14
  150.0 49.4 all-gather.22
  201.5 39.9 all-gather.16
  243.4 37.7 all-gather.30
  283.4 39.0 all-gather.28
  324.6 41.4 all-gather.20
  368.3 73.6 all-gather.24
  444.0 73.1 all-gather.26
  652.5 35.8 reduce-scatter.22
  690.5 37.5 reduce-scatter.24
  743.8 9.7 reduce-scatter.58
  755.7 31.8 reduce-scatter.38
  789.7 31.8 reduce-scatter.34
  823.7 31.8 reduce-scatter.26
  857.7 31.8 reduce-scatter.30
  891.8 54.2 reduce-scatter.54
  948.5 54.3 reduce-scatter.50
  1005.0 99.2 reduce-scatter.42
  1106.7 99.2 reduce-scatter.46
  1210.0 55.0 reduce-scatter.60
  1268.7 56.3 reduce-scatter.40
  1329.0 56.4 reduce-scatter.36
  1389.2 56.3 reduce-scatter.28
  1449.5 56.4 reduce-scatter.32
  1509.5 60.5 reduce-scatter.56
  1574.3 60.5 reduce-scatter.52
  1638.8 71.5 reduce-scatter.44
  1714.5 71.3 reduce-scatter.48
where the time goes:
time: 1800 us; the launch traced here: 1790 us
  waiting for transfers between devices  1310 us (73%)
  matrix products  288 us (16%)
  other arithmetic  117 us (6%)
  local copies, waits for them, and re-layouts  60.6 us (3%)
    reduce_scatter x1, waiting for transfers between devices, shards(): lax.psum_scatter(part_down.astype(jnp.bfloat16), 'seq', scatter_dimension...  101 us
    reduce_scatter x1, waiting for transfers between devices, shards(): lax.psum_scatter(part_up.astype(jnp.bfloat16), 'seq', scatter_dimension=0...  101 us
    reduce_scatter x1, waiting for transfers between devices, shards(): lax.psum_scatter(seq_up.astype(jnp.bfloat16), 'items', scatter_dimension=...  73.8 us
    reduce_scatter x1, waiting for transfers between devices, shards(): lax.psum_scatter(seq_down.astype(jnp.bfloat16), 'items', scatter_dimensio...  73.8 us
    all_gather x1, waiting for transfers between devices, shards(): lax.all_gather(w_up, 'items', axis=0, tiled=True)  70.7 us
    reduce_scatter x1, waiting for transfers between devices, shards(): lax.psum_scatter(seq_ada_one.astype(jnp.bfloat16), 'items', scatter_dimen...  63.1 us
    reduce_scatter x1, waiting for transfers between devices, shards(): lax.psum_scatter(seq_ada_two.astype(jnp.bfloat16), 'items', scatter_dimen...  62.7 us
    reduce_scatter x1, waiting for transfers between devices, shards(): lax.psum_scatter(seq_value.astype(jnp.bfloat16), 'items', scatter_dimensi...  58.9 us
  transfers between devices with their start and end apart: 30, of which 25 were waited for; matrix products, arithmetic and copies ran while one was open for 17% of the time, Pallas kernels for 0%

commit v1 on v0

--- a/solution.py
+++ b/solution.py
@@ -10,6 +10,18 @@
 PROMPT = 640
 EPSILON = 1e-05
 MASKED = -1e30
+
+
+def collect(x, axis, dim):
+    ways, here, step = (lax.axis_size(axis), lax.axis_index(axis), x.shape[dim])
+    line, have = (x, 1)
+    while have < ways:
+        line = jnp.concatenate(
+            [line, lax.ppermute(line, axis, [(d, (d - have) % ways) for d in range(ways)])],
+            axis=dim,
+        )
+        have = 2 * have
+    return jnp.roll(line, here * step, axis=dim)
 
 
 def exact(left, right):
@@ -70,7 +82,7 @@
         lax.all_gather(w_up, "items", axis=0, tiled=True),
         lax.all_gather(w_down, "items", axis=0, tiled=True),
         lax.all_gather(w_ada_one, "items", axis=0, tiled=True),
-        lax.all_gather(w_ada_two, "items", axis=0, tiled=True),
+        collect(w_ada_two, "items", 0),
     )
     batch, rows, width = tokens.shape
     items_count = lax.axis_size("items")

time: 1800 us -> 1770 us (0.983)
  waiting for transfers between devices: 1310 us -> 1260 us
    ppermute x0 -> x4, waiting for transfers between devices: none -> 143 us  [collect(): lax.ppermute(line, axis, [(d, (d - have) % ways) for d in range(ways)])]
    all_gather x1, waiting for transfers between devices: 70.7 us -> 19 us  [shards(): lax.all_gather(w_up, 'items', axis=0, tiled=True)]
    all_gather x1 -> x0, waiting for transfers between devices: 43.8 us -> none  [shards(): lax.all_gather(w_ada_two, 'items', axis=0, tiled=True)]
    all_gather x1, waiting for transfers between devices: 38 us -> 0.01 us  [shards(): lax.all_gather(w_query, 'items', axis=0, tiled=True)]
    all_gather x1, waiting for transfers between devices: 35.2 us -> 0.01 us  [shards(): lax.all_gather(keys_here, 'seq', axis=1, tiled=True)]
    unnamed x31 -> x30, waiting for transfers between devices: 53.1 us -> 52.1 us
  transfers between devices with their start and end apart: 30 -> 33, of which waited for: 25 -> 25; matrix products, arithmetic and copies ran while one was open for 17% -> 18% of each run, Pallas kernels for 0% -> 0%
where the time goes in v1:
time: 1770 us; the launch traced here: 1760 us
  waiting for transfers between devices  1260 us (71%)
  matrix products  289 us (16%)
  other arithmetic  121 us (7%)
  local copies, waits for them, and re-layouts  69 us (4%)
    ppermute x4, waiting for transfers between devices, collect(): lax.ppermute(line, axis, [(d, (d - have) % ways) for d in range(ways)])  143 us
    reduce_scatter x1, waiting for transfers between devices, shards(): lax.psum_scatter(part_up.astype(jnp.bfloat16), 'seq', scatter_dimension=0...  101 us
    reduce_scatter x1, waiting for transfers between devices, shards(): lax.psum_scatter(part_down.astype(jnp.bfloat16), 'seq', scatter_dimension...  101 us
    reduce_scatter x1, waiting for transfers between devices, shards(): lax.psum_scatter(seq_down.astype(jnp.bfloat16), 'items', scatter_dimensio...  74 us
    reduce_scatter x1, waiting for transfers between devices, shards(): lax.psum_scatter(seq_up.astype(jnp.bfloat16), 'items', scatter_dimension=...  73.9 us
    reduce_scatter x1, waiting for transfers between devices, shards(): lax.psum_scatter(seq_ada_one.astype(jnp.bfloat16), 'items', scatter_dimen...  63 us
    reduce_scatter x1, waiting for transfers between devices, shards(): lax.psum_scatter(seq_ada_two.astype(jnp.bfloat16), 'items', scatter_dimen...  62.7 us
    reduce_scatter x1, waiting for transfers between devices, shards(): lax.psum_scatter(seq_value.astype(jnp.bfloat16), 'items', scatter_dimensi...  59 us
  transfers between devices with their start and end apart: 33, of which 25 were waited for; matrix products, arithmetic and copies ran while one was open for 18% of the time, Pallas kernels for 0%

profile of v1, /device:TPU:0, one launch (start us, length us, event | category | flops | bytes accessed | tf_op | source)
XLA Modules:
  0.0 1763.7 jit_solution(14501842766483960624)
XLA Ops:
  14.2 49.3 %all-gather.12.cloned.1.call-done = bf16[1024,2048]{1,0:T(8,128)(2,1)} async-done(((bf16[64,2048]{1,0:T(8,128)(2,1)}), bf16[1024,2048]{1,0:T(8,128)(2,1)}) %all-gather.12.cloned.1.call-update) | async-done | bytes 4194320 | tf_op jit(solution)/shard_map/all_gather | solution.py:84
  63.5 3.9 fusion.77
  67.4 38.1 %all-gather.18.cloned.1.call-done = bf16[1024,1024]{1,0:T(8,128)(2,1)} async-done(((bf16[64,1024]{1,0:T(8,128)(2,1)}), bf16[1024,1024]{1,0:T(8,128)(2,1)}) %all-gather.18.cloned.1.call-update) | async-done | bytes 2097168 | tf_op jit(solution)/shard_map/all_gather | solution.py:79
  105.6 4.2 convolution_convert_fusion.1
  109.9 38.0 %all-gather.14.cloned.1.call-done = bf16[1024,1024]{1,0:T(8,128)(2,1)} async-done(((bf16[64,1024]{1,0:T(8,128)(2,1)}), bf16[1024,1024]{1,0:T(8,128)(2,1)}) %all-gather.14.cloned.1.call-update) | async-done | bytes 2097168 | tf_op jit(solution)/shard_map/all_gather | solution.py:80
  148.0 4.2 convolution_convert_fusion.3
  155.8 5.4 collective-permute-done
  161.3 14.2 collective-permute-done.1
  175.7 33.8 %collective-permute-done.2 = bf16[256,2048]{1,0:T(8,128)(2,1)S(1)} collective-permute-done((bf16[256,2048]{1,0:T(8,128)(2,1)S(1)}, bf16[256,2048]{1,0:T(8,128)(2,1)S(1)}, u32[]{:S(2)}, u32[]{:S(2)}) %collective-permute-start.2) | collective-permute-done | bytes 1048608 | tf_op jit(solution)/shard_map/ppermute | solution.py:20
  215.1 89.1 %collective-permute-done.3 = bf16[512,2048]{1,0:T(8,128)(2,1)} collective-permute-done((bf16[512,2048]{1,0:T(8,128)(2,1)}, bf16[512,2048]{1,0:T(8,128)(2,1)}, u32[]{:S(2)}, u32[]{:S(2)}) %collective-permute-start.3) | collective-permute-done | bytes 2097184 | tf_op jit(solution)/shard_map/ppermute | solution.py:20
  307.9 3.2 copy-done.11
  313.0 3.2 convolution_convert_fusion.2
  317.8 3.2 copy.60
  321.0 22.7 %fusion.97 = (f32[16,640]{1,0:T(8,128)S(1)}, f32[16,640,1280]{2,1,0:T(8,128)}) fusion(bf16[640,16,64]{0,2,1:T(8,128)(2,1)} %bitcast.282, bf16[1280,16,64]{0,2,1:T(8,128)(2,1)S(1)} %bitcast.276, pred[640,1280]{1,0:T(8,128)(4,1)S(1)} %and_or_fusion), kind=kOutput, calls=%fused_computation.170 | convolution fusion | flops 1717032960 | bytes 57221120 | tf_op jit(solution)/shard_map/while/body/eval_jaxpr/qhd,khd->hqk/dot_general | solution.py:127
  343.7 17.2 fusion
  360.9 4.4 copy.58
  365.3 20.9 %fusion.54 = bf16[16,64,640]{2,1,0:T(8,128)(2,1)S(1)} fusion(bf16[1280,16,64]{0,2,1:T(8,128)(2,1)} %bitcast.287, f32[16,640,1280]{2,1,0:T(8,128)} %get-tuple-element.90, f32[16,640]{1,0:T(8,128)S(1)} %fusion, f32[16,640]{1,0:T(8,128)S(1)} %get-tuple-element.89), kind=kOutput, calls=%fused_computation.102 | convolution fusion | flops 1717698560 | bytes 56442880 | tf_op jit(solution)/shard_map/while/body/eval_jaxpr/hqk,khd->qhd/dot_general | solution.py:147
  386.3 3.7 fusion.98
  392.0 19.0 %all-gather.22.cloned.1.call-done = bf16[1024,4096]{1,0:T(8,128)(2,1)} async-done(((bf16[64,4096]{1,0:T(8,128)(2,1)}), bf16[1024,4096]{1,0:T(8,128)(2,1)}) %all-gather.22.cloned.1.call-update) | async-done | bytes 8388624 | tf_op jit(solution)/shard_map/all_gather | solution.py:82
  411.0 32.4 %fusion.6 = (f32[640,4096]{1,0:T(8,128)}, f32[640,4096]{1,0:T(8,128)}) fusion(bf16[1024,4096]{1,0:T(8,128)(2,1)} %all-gather.22.cloned.1.call-done, f32[1024]{0:T(1024)S(1)} %bitcast.328, f32[640]{0:T(1024)S(1)} %fusion.80, f32[1,640,1024]{2,1,0:T(8,128)} %copy-done.6, f32[640]{0:T(1024)S(1)} %broadcast_multiply_fusion, f32[1024]{0:T(1024)S(1)} %bitcast.308), kind=kOutput, calls=%fused_computation.13 | convolution fusion | flops 5534515200 | bytes 31994880 | tf_op jit(solution)/shard_map/dot_general | solution.py:162
  443.4 43.0 %all-gather.24.cloned.1.call-done = bf16[4096,1024]{1,0:T(8,128)(2,1)} async-done(((bf16[256,1024]{1,0:T(8,128)(2,1)}), bf16[4096,1024]{1,0:T(8,128)(2,1)}) %all-gather.24.cloned.1.call-update) | async-done | bytes 8388624 | tf_op jit(solution)/shard_map/all_gather | solution.py:83
  486.3 16.7 add_convert_fusion
  503.1 10.2 fusion.99
  513.3 2.1 fusion.50
  521.6 38.6 %multiply_reduce_fusion = (f32[16,640]{1,0:T(8,128)S(1)}, f32[16,640,1280]{2,1,0:T(8,128)}) fusion(f32[16,640,1280]{2,1,0:T(8,128)} %get-tuple-element.90, f32[16,640]{1,0:T(8,128)S(1)} %log_add_fusion, bf16[640,16,64]{0,2,1:T(8,128)(2,1)S(1)} %bitcast.285, bf16[1280,16,64]{0,2,1:T(8,128)(2,1)} %bitcast.288), kind=kOutput, calls=%fused_computation.1 | convolution fusion | flops 1717032960 | bytes 108871680 | tf_op jit(solution)/shard_map/while/body/eval_jaxpr/qhd,khd->hqk/dot_general | solution.py:191
  560.2 42.2 %multiply_convert_fusion = bf16[16,640,1280]{2,1,0:T(8,128)(2,1)} fusion(f32[16,640,1280]{2,1,0:T(8,128)} %get-tuple-element.96, f32[16,640,1280]{2,1,0:T(8,128)} %get-tuple-element.90, f32[16,640]{1,0:T(8,128)S(1)} %get-tuple-element.95, f32[16,640]{1,0:T(8,128)S(1)} %log_add_fusion), kind=kLoop, calls=%fused_computation | loop fusion | flops 52428800 | bytes 131153920 | tf_op jit(solution)/shard_map/while/body/eval_jaxpr/convert_element_type | solution.py:195
  602.5 14.6 multiply_convert_fusion.5
  617.1 4.5 copy.62
  621.7 21.5 %fusion.36 = bf16[16,64,1280]{2,1,0:T(8,128)(2,1)} fusion(bf16[640,16,64]{0,2,1:T(8,128)(2,1)S(1)} %bitcast.286, f32[16,640,1280]{2,1,0:T(8,128)} %get-tuple-element.90, f32[16,640]{1,0:T(8,128)S(1)} %log_add_fusion), kind=kOutput, calls=%fused_computation.67 | convolution fusion | flops 1705246720 | bytes 56401920 | tf_op jit(solution)/shard_map/while/body/eval_jaxpr/hqk,qhd->khd/dot_general | solution.py:221
  643.1 4.5 copy.63
  647.8 5.7 fusion.39
  653.5 14.9 multiply_convert_fusion.6
  668.3 5.2 fusion.100
  673.5 4.4 fusion.60
  677.9 19.7 %reduce-scatter.25.cloned.1.call-done = bf16[1,640,1024]{2,1,0:T(8,128)(2,1)} async-done(((bf16[1,1280,1024]{2,1,0:T(8,128)(2,1)}), bf16[1,640,1024]{2,1,0:T(8,128)(2,1)}) %reduce-scatter.25.cloned.1.call-update) | async-done | bytes 1310736 | tf_op jit(solution)/shard_map/reduce_scatter | solution.py:240
  697.6 5.9 fusion.49
  703.7 2.5 fusion.47
  706.1 5.5 fusion.74
  713.1 3.5 convert_bitcast_fusion.2
  718.2 4.5 fusion.94
  724.4 3.1 convert_bitcast_fusion.3
  736.7 6.5 multiply_convert_fusion.2
  745.2 11.5 convert_bitcast_fusion.1
  756.8 7.8 copy.71
  764.6 24.6 %fusion.9 = bf16[4096,640]{0,1:T(8,128)(2,1)} fusion(f32[640,4096]{1,0:T(8,128)} %get-tuple-element.94), kind=kLoop, calls=%fused_computation.16 | loop fusion | flops 170393600 | bytes 15728640 | tf_op jit(solution)/shard_map/convert_element_type | solution.py:164
  789.2 7.9 copy.83
  797.1 12.2 convert_bitcast_fusion
  809.3 8.2 copy.73
  820.7 4.0 reduce-scatter.27.cloned.1.call-done
  824.8 34.0 %reduce-scatter.31.cloned.1.call-done = bf16[512,1024]{1,0:T(8,128)(2,1)} async-done(((bf16[1024,1024]{1,0:T(8,128)(2,1)}), bf16[512,1024]{1,0:T(8,128)(2,1)}) %reduce-scatter.31.cloned.1.call-update) | async-done | bytes 1048592 | tf_op jit(solution)/shard_map/reduce_scatter | solution.py:283
  858.8 56.4 %reduce-scatter.55.cloned.1.call-done = bf16[512,2048]{1,0:T(8,128)(2,1)} async-done(((bf16[1024,2048]{1,0:T(8,128)(2,1)}), bf16[512,2048]{1,0:T(8,128)(2,1)}) %reduce-scatter.55.cloned.1.call-update) | async-done | bytes 2097168 | tf_op jit(solution)/shard_map/reduce_scatter | solution.py:301
  915.3 56.5 %reduce-scatter.51.cloned.1.call-done = bf16[512,2048]{1,0:T(8,128)(2,1)} async-done(((bf16[1024,2048]{1,0:T(8,128)(2,1)}), bf16[512,2048]{1,0:T(8,128)(2,1)}) %reduce-scatter.51.cloned.1.call-update) | async-done | bytes 2097168 | tf_op jit(solution)/shard_map/reduce_scatter | solution.py:298
  971.9 101.5 %reduce-scatter.43.cloned.1.call-done = bf16[512,4096]{1,0:T(8,128)(2,1)} async-done(((bf16[1024,4096]{1,0:T(8,128)(2,1)}), bf16[512,4096]{1,0:T(8,128)(2,1)}) %reduce-scatter.43.cloned.1.call-update) | async-done | bytes 4194320 | tf_op jit(solution)/shard_map/reduce_scatter | solution.py:292
  1073.6 101.3 %reduce-scatter.47.cloned.1.call-done = bf16[2048,1024]{1,0:T(8,128)(2,1)} async-done(((bf16[4096,1024]{1,0:T(8,128)(2,1)}), bf16[2048,1024]{1,0:T(8,128)(2,1)}) %reduce-scatter.47.cloned.1.call-update) | async-done | bytes 4194320 | tf_op jit(solution)/shard_map/reduce_scatter | solution.py:295
  1174.9 13.2 fusion.52
  1188.1 46.0 %reduce-scatter.61.cloned.1.call-done = bf16[32,8]{1,0:T(8,128)(2,1)} async-done(((bf16[512,8]{1,0:T(8,128)(2,1)}), bf16[32,8]{1,0:T(8,128)(2,1)}) %reduce-scatter.61.cloned.1.call-update) | async-done | bytes 528
  1235.4 58.7 %reduce-scatter.41.cloned.1.call-done = bf16[32,1024]{1,0:T(8,128)(2,1)} async-done(((bf16[512,1024]{1,0:T(8,128)(2,1)}), bf16[32,1024]{1,0:T(8,128)(2,1)}) %reduce-scatter.41.cloned.1.call-update) | async-done | bytes 65552 | tf_op jit(solution)/shard_map/reduce_scatter | solution.py:328
  1295.7 59.0 %reduce-scatter.37.cloned.1.call-done = bf16[32,1024]{1,0:T(8,128)(2,1)} async-done(((bf16[512,1024]{1,0:T(8,128)(2,1)}), bf16[32,1024]{1,0:T(8,128)(2,1)}) %reduce-scatter.37.cloned.1.call-update) | async-done | bytes 65552 | tf_op jit(solution)/shard_map/reduce_scatter | solution.py:325
  1356.1 58.5 %reduce-scatter.29.cloned.1.call-done = bf16[32,1024]{1,0:T(8,128)(2,1)} async-done(((bf16[512,1024]{1,0:T(8,128)(2,1)}), bf16[32,1024]{1,0:T(8,128)(2,1)}) %reduce-scatter.29.cloned.1.call-update) | async-done | bytes 65552 | tf_op jit(solution)/shard_map/reduce_scatter | solution.py:319
  1416.1 59.0 %reduce-scatter.33.cloned.1.call-done = bf16[32,1024]{1,0:T(8,128)(2,1)} async-done(((bf16[512,1024]{1,0:T(8,128)(2,1)}), bf16[32,1024]{1,0:T(8,128)(2,1)}) %reduce-scatter.33.cloned.1.call-update) | async-done | bytes 65552 | tf_op jit(solution)/shard_map/reduce_scatter | solution.py:322
  1476.6 62.7 %reduce-scatter.57.cloned.1.call-done = bf16[32,2048]{1,0:T(8,128)(2,1)} async-done(((bf16[512,2048]{1,0:T(8,128)(2,1)}), bf16[32,2048]{1,0:T(8,128)(2,1)}) %reduce-scatter.57.cloned.1.call-update) | async-done | bytes 131088 | tf_op jit(solution)/shard_map/reduce_scatter | solution.py:340
  1540.9 63.0 %reduce-scatter.53.cloned.1.call-done = bf16[32,2048]{1,0:T(8,128)(2,1)} async-done(((bf16[512,2048]{1,0:T(8,128)(2,1)}), bf16[32,2048]{1,0:T(8,128)(2,1)}) %reduce-scatter.53.cloned.1.call-update) | async-done | bytes 131088 | tf_op jit(solution)/shard_map/reduce_scatter | solution.py:337
  1605.5 73.9 %reduce-scatter.45.cloned.1.call-done = bf16[32,4096]{1,0:T(8,128)(2,1)} async-done(((bf16[512,4096]{1,0:T(8,128)(2,1)}), bf16[32,4096]{1,0:T(8,128)(2,1)}) %reduce-scatter.45.cloned.1.call-update) | async-done | bytes 262160 | tf_op jit(solution)/shard_map/reduce_scatter | solution.py:331
  1681.2 74.0 %reduce-scatter.49.cloned.1.call-done = bf16[128,1024]{1,0:T(8,128)(2,1)} async-done(((bf16[2048,1024]{1,0:T(8,128)(2,1)}), bf16[128,1024]{1,0:T(8,128)(2,1)}) %reduce-scatter.49.cloned.1.call-update) | async-done | bytes 262160 | tf_op jit(solution)/shard_map/reduce_scatter | solution.py:334
  (212 shorter events, 64.0 us)
Async XLA Ops:
  7.2 6.9 copy-start
  7.2 98.4 %copy-start.4 = (bf16[1,640,1024]{2,1,0:T(8,128)(2,1)S(1)}, bf16[1,640,1024]{2,1,0:T(8,128)(2,1)}, u32[]{:S(2)}) copy-start(bf16[1,640,1024]{2,1,0:T(8,128)(2,1)} %param.13) | copy-start | bytes 3932164
  7.2 56.3 %all-gather.12.cloned.1.call-start = ((), (), s32[]{:S(2)}) async-start(), calls=%async_computation.20 | async-start | bytes 4456448 | tf_op jit(solution)/shard_map/all_gather | solution.py:84
  7.9 97.6 %all-gather.18.cloned.1.call-start = ((), (), s32[]{:S(2)}) async-start(), calls=%async_computation.23 | async-start | bytes 2228224 | tf_op jit(solution)/shard_map/all_gather | solution.py:79
  8.7 139.3 %all-gather.14.cloned.1.call-start = ((), (), s32[]{:S(2)}) async-start(), calls=%async_computation.21 | async-start | bytes 2228224 | tf_op jit(solution)/shard_map/all_gather | solution.py:80
  9.4 303.5 %all-gather.16.cloned.1.call-start = ((), (), s32[]{:S(2)}) async-start(), calls=%async_computation.22 | async-start | bytes 2228224 | tf_op jit(solution)/shard_map/all_gather | solution.py:78
  10.0 307.8 %all-gather.28.cloned.1.call-start = ((), (), s32[]{:S(2)}) async-start(), calls=%async_computation.47 | async-start | bytes 3932160 | tf_op jit(solution)/shard_map/all_gather | solution.py:121
  12.3 300.7 %copy-start.22 = (f32[640]{0:T(1024)}, f32[640]{0:T(1024)S(1)}, u32[]{:S(2)}) copy-start(f32[640]{0:T(1024)S(1)} %broadcast_multiply_fusion.1) | copy-start | bytes 7684
  14.1 95.8 %copy-start.30 = (f32[640]{0:T(1024)}, f32[640]{0:T(1024)S(1)}, u32[]{:S(2)}) copy-start(f32[640]{0:T(1024)S(1)} %fusion.48) | copy-start | bytes 7684
  14.1 298.8 %copy-start.26 = (f32[640]{0:T(1024)}, f32[640]{0:T(1024)S(1)}, u32[]{:S(2)}) copy-start(f32[640]{0:T(1024)S(1)} %fusion.79) | copy-start | bytes 7684
  14.2 293.6 %copy-start.28 = (f32[1,1024]{1,0:T(1,128)}, f32[1,1024]{1,0:T(1,128)S(1)}, u32[]{:S(2)}) copy-start(f32[1,1024]{1,0:T(1,128)S(1)} %fusion.81) | copy-start | bytes 12292
  67.4 245.5 %copy-start.24 = (f32[1,1024]{1,0:T(1,128)}, f32[1,1024]{1,0:T(1,128)S(1)}, u32[]{:S(2)}) copy-start(f32[1,1024]{1,0:T(1,128)S(1)} %get-tuple-element.87) | copy-start | bytes 12292
  67.4 245.5 %copy-start.32 = (f32[1,1024]{1,0:T(1,128)}, f32[1,1024]{1,0:T(1,128)S(1)}, u32[]{:S(2)}) copy-start(f32[1,1024]{1,0:T(1,128)S(1)} %get-tuple-element.88) | copy-start | bytes 12292
  109.8 43.9 %copy-start.14 = (bf16[64,2048]{1,0:T(8,128)(2,1)S(1)}, bf16[64,2048]{1,0:T(8,128)(2,1)}, u32[]{:S(2)}) copy-start(bf16[64,2048]{1,0:T(8,128)(2,1)} %param.25) | copy-start | bytes 786436
  109.9 251.0 %all-gather.26.cloned.1.call-start = ((), (), s32[]{:S(2)}) async-start(), calls=%async_computation.46 | async-start | bytes 3932160 | tf_op jit(solution)/shard_map/all_gather | solution.py:122
  152.2 234.1 %all-gather.20.cloned.1.call-start = ((), (), s32[]{:S(2)}) async-start(), calls=%async_computation.24 | async-start | bytes 2228224 | tf_op jit(solution)/shard_map/all_gather | solution.py:81
  153.0 258.0 %all-gather.22.cloned.1.call-start = ((), (), s32[]{:S(2)}) async-start(), calls=%async_computation.25 | async-start | bytes 8912896 | tf_op jit(solution)/shard_map/all_gather | solution.py:82
  153.7 332.6 %all-gather.24.cloned.1.call-start = ((), (), s32[]{:S(2)}) async-start(), calls=%async_computation.26 | async-start | bytes 8912896 | tf_op jit(solution)/shard_map/all_gather | solution.py:83
  153.8 7.4 collective-permute-start
  161.1 49.8 %copy-start.15 = (bf16[64,2048]{1,0:T(8,128)(2,1)}, bf16[64,2048]{1,0:T(8,128)(2,1)S(1)}, u32[]{:S(2)}) copy-start(bf16[64,2048]{1,0:T(8,128)(2,1)S(1)} %collective-permute-done) | copy-start | bytes 786436
  161.2 14.3 collective-permute-start.1
  175.5 34.0 %copy-start.12 = (bf16[128,2048]{1,0:T(8,128)(2,1)}, bf16[128,2048]{1,0:T(8,128)(2,1)S(1)}, u32[]{:S(2)}) copy-start(bf16[128,2048]{1,0:T(8,128)(2,1)S(1)} %collective-permute-done.1) | copy-start | bytes 1572868
  175.6 33.9 %collective-permute-start.2 = (bf16[256,2048]{1,0:T(8,128)(2,1)S(1)}, bf16[256,2048]{1,0:T(8,128)(2,1)S(1)}, u32[]{:S(2)}, u32[]{:S(2)}) collective-permute-start(bf16[256,2048]{1,0:T(8,128)(2,1)S(1)} %pad_maximum_fusion.1), channel_id=1, source_target_pairs={{0,24},{2,26},{4,28},{6,30},{8,0},{10,2},{12,4},{14,6},{16,8},{18,... | collective-permute-start | bytes 3145736 | tf_op jit(solution)/shard_map/ppermute | solution.py:20
  210.9 93.3 %collective-permute-start.3 = (bf16[512,2048]{1,0:T(8,128)(2,1)}, bf16[512,2048]{1,0:T(8,128)(2,1)}, u32[]{:S(2)}, u32[]{:S(2)}) collective-permute-start(bf16[512,2048]{1,0:T(8,128)(2,1)} %pad_maximum_fusion), channel_id=1, source_target_pairs={{0,16},{2,18},{4,20},{6,22},{8,24},{10,26},{12,28},{14,30},{16,0},... | collective-permute-start | bytes 6291464 | tf_op jit(solution)/shard_map/ppermute | solution.py:20
  211.5 462.0 %reduce-scatter.23.cloned.1.call-start = ((), (), s32[]{:S(2)}) async-start(), calls=%async_computation.27 | async-start | bytes 3932160 | tf_op jit(solution)/shard_map/reduce_scatter | solution.py:237
  212.8 93.2 %copy-start.16 = (bf16[64,2048]{1,0:T(8,128)(2,1)S(1)}, bf16[64,2048]{1,0:T(8,128)(2,1)}, u32[]{:S(2)}) copy-start(bf16[64,2048]{1,0:T(8,128)(2,1)} %copy-done.15) | copy-start | bytes 786436
  213.8 92.2 %copy-start.13 = (bf16[128,2048]{1,0:T(8,128)(2,1)S(1)}, bf16[128,2048]{1,0:T(8,128)(2,1)}, u32[]{:S(2)}) copy-start(bf16[128,2048]{1,0:T(8,128)(2,1)} %copy-done.12) | copy-start | bytes 1572868
  307.9 3.3 copy-start.11
  321.0 22.7 %copy-start.2 = (bf16[1280,1024]{0,1:T(8,128)(2,1)}, bf16[1280,1024]{0,1:T(8,128)(2,1)S(1)}, u32[]{:S(2)}) copy-start(bf16[1280,1024]{0,1:T(8,128)(2,1)S(1)} %copy.60) | copy-start | bytes 7864324
  365.3 21.0 %copy-start.5 = (bf16[1,640,1024]{2,1,0:T(8,128)(2,1)S(1)}, bf16[1,640,1024]{2,1,0:T(8,128)(2,1)}, u32[]{:S(2)}) copy-start(bf16[1,640,1024]{2,1,0:T(8,128)(2,1)} %param.13) | copy-start | bytes 3932164
  386.2 3.7 copy-start.37
  411.0 75.3 %copy-start.18 = (bf16[1,640,1024]{2,1,0:T(8,128)(2,1)S(1)}, bf16[1,640,1024]{2,1,0:T(8,128)(2,1)}, u32[]{:S(2)}) copy-start(bf16[1,640,1024]{2,1,0:T(8,128)(2,1)} %param.14) | copy-start | bytes 3932164
  503.1 10.3 copy-start.7
  516.3 2.9 copy-start.35
  560.2 42.2 %copy-start.10 = (bf16[640,1024]{0,1:T(8,128)(2,1)S(1)}, bf16[640,1024]{0,1:T(8,128)(2,1)}, u32[]{:S(2)}) copy-start(bf16[640,1024]{0,1:T(8,128)(2,1)} %copy.59) | copy-start | bytes 3932164
  621.6 76.0 %reduce-scatter.25.cloned.1.call-start = ((), (), s32[]{:S(2)}) async-start(), calls=%async_computation.28 | async-start | bytes 3932160 | tf_op jit(solution)/shard_map/reduce_scatter | solution.py:240
  647.7 5.8 copy-start.3
  647.7 169.9 %reduce-scatter.59.cloned.1.call-start = ((), (), s32[]{:S(2)}) async-start(), calls=%async_computation.45 | async-start | bytes 24576 | tf_op jit(solution)/shard_map/reduce_scatter | solution.py:304
  668.3 5.2 copy-start.34
  673.5 24.1 %copy-start.23 = (f32[640]{0:T(1024)S(1)}, f32[640]{0:T(1024)}, u32[]{:S(2)}) copy-start(f32[640]{0:T(1024)} %copy-done.22) | copy-start | bytes 7684
  673.5 24.1 %copy-start.25 = (f32[1,1024]{1,0:T(1,128)S(1)}, f32[1,1024]{1,0:T(1,128)}, u32[]{:S(2)}) copy-start(f32[1,1024]{1,0:T(1,128)} %copy-done.24) | copy-start | bytes 12292
  677.9 25.6 %copy-start.31 = (f32[640]{0:T(1024)S(1)}, f32[640]{0:T(1024)}, u32[]{:S(2)}) copy-start(f32[640]{0:T(1024)} %copy-done.30) | copy-start | bytes 7684
  677.9 25.8 %copy-start.27 = (f32[640]{0:T(1024)S(1)}, f32[640]{0:T(1024)}, u32[]{:S(2)}) copy-start(f32[640]{0:T(1024)} %copy-done.26) | copy-start | bytes 7684
  712.6 106.6 %reduce-scatter.39.cloned.1.call-start = ((), (), s32[]{:S(2)}) async-start(), calls=%async_computation.35 | async-start | bytes 3145728 | tf_op jit(solution)/shard_map/reduce_scatter | solution.py:289
  718.1 101.9 %reduce-scatter.35.cloned.1.call-start = ((), (), s32[]{:S(2)}) async-start(), calls=%async_computation.33 | async-start | bytes 3145728 | tf_op jit(solution)/shard_map/reduce_scatter | solution.py:286
  729.1 95.6 %reduce-scatter.27.cloned.1.call-start = ((), (), s32[]{:S(2)}) async-start(), calls=%async_computation.29 | async-start | bytes 3145728 | tf_op jit(solution)/shard_map/reduce_scatter | solution.py:280
  731.2 2.0 copy-start.36
  732.7 126.0 %reduce-scatter.31.cloned.1.call-start = ((), (), s32[]{:S(2)}) async-start(), calls=%async_computation.31 | async-start | bytes 3145728 | tf_op jit(solution)/shard_map/reduce_scatter | solution.py:283
  736.6 178.7 %reduce-scatter.55.cloned.1.call-start = ((), (), s32[]{:S(2)}) async-start(), calls=%async_computation.43 | async-start | bytes 6291456 | tf_op jit(solution)/shard_map/reduce_scatter | solution.py:301
  743.2 228.6 %reduce-scatter.51.cloned.1.call-start = ((), (), s32[]{:S(2)}) async-start(), calls=%async_computation.41 | async-start | bytes 6291456 | tf_op jit(solution)/shard_map/reduce_scatter | solution.py:298
  743.8 329.5 %reduce-scatter.43.cloned.1.call-start = ((), (), s32[]{:S(2)}) async-start(), calls=%async_computation.37 | async-start | bytes 12582912 | tf_op jit(solution)/shard_map/reduce_scatter | solution.py:292
  764.5 410.4 %reduce-scatter.47.cloned.1.call-start = ((), (), s32[]{:S(2)}) async-start(), calls=%async_computation.39 | async-start | bytes 12582912 | tf_op jit(solution)/shard_map/reduce_scatter | solution.py:295
  789.2 7.9 copy-start.19
  817.6 416.5 %reduce-scatter.61.cloned.1.call-start = ((), (), s32[]{:S(2)}) async-start(), calls=%async_computation.48 | async-start | bytes 139264
  819.2 475.0 %reduce-scatter.41.cloned.1.call-start = ((), (), s32[]{:S(2)}) async-start(), calls=%async_computation.36 | async-start | bytes 1114112 | tf_op jit(solution)/shard_map/reduce_scatter | solution.py:328
  819.9 534.7 %reduce-scatter.37.cloned.1.call-start = ((), (), s32[]{:S(2)}) async-start(), calls=%async_computation.34 | async-start | bytes 1114112 | tf_op jit(solution)/shard_map/reduce_scatter | solution.py:325
  820.6 594.0 %reduce-scatter.29.cloned.1.call-start = ((), (), s32[]{:S(2)}) async-start(), calls=%async_computation.30 | async-start | bytes 1114112 | tf_op jit(solution)/shard_map/reduce_scatter | solution.py:319
  824.7 650.4 %reduce-scatter.33.cloned.1.call-start = ((), (), s32[]{:S(2)}) async-start(), calls=%async_computation.32 | async-start | bytes 1114112 | tf_op jit(solution)/shard_map/reduce_scatter | solution.py:322
  858.8 680.5 %reduce-scatter.57.cloned.1.call-start = ((), (), s32[]{:S(2)}) async-start(), calls=%async_computation.44 | async-start | bytes 2228224 | tf_op jit(solution)/shard_map/reduce_scatter | solution.py:340
  915.2 688.7 %reduce-scatter.53.cloned.1.call-start = ((), (), s32[]{:S(2)}) async-start(), calls=%async_computation.42 | async-start | bytes 2228224 | tf_op jit(solution)/shard_map/reduce_scatter | solution.py:337
  971.8 707.6 %reduce-scatter.45.cloned.1.call-start = ((), (), s32[]{:S(2)}) async-start(), calls=%async_computation.38 | async-start | bytes 4456448 | tf_op jit(solution)/shard_map/reduce_scatter | solution.py:331
  1073.4 101.6 %copy-start.8 = (f32[1,640,1024]{2,1,0:T(8,128)S(1)}, f32[1,640,1024]{2,1,0:T(8,128)}, u32[]{:S(2)}) copy-start(f32[1,640,1024]{2,1,0:T(8,128)} %copy-done.6) | copy-start | bytes 7864324
  1073.4 681.8 %reduce-scatter.49.cloned.1.call-start = ((), (), s32[]{:S(2)}) async-start(), calls=%async_computation.40 | async-start | bytes 4456448 | tf_op jit(solution)/shard_map/reduce_scatter | solution.py:334
  1174.9 582.0 %copy-start.1 = (bf16[8,1024]{1,0:T(8,128)(2,1)S(1)}, bf16[8,1024]{1,0:T(8,128)(2,1)}, u32[]{:S(2)}) copy-start(bf16[8,1024]{1,0:T(8,128)(2,1)} %param.17) | copy-start | bytes 49156
  (7 other events, 10.4 us)
Sparse Core Ops, SparseCore 0:
  10.2 53.2 all-gather.11
  65.7 39.8 all-gather.17
  107.7 40.1 all-gather.13
  150.0 52.2 all-gather.15
  203.7 46.1 all-gather.27
  251.8 39.0 all-gather.25
  293.1 42.0 all-gather.19
  337.3 73.6 all-gather.21
  413.2 73.1 all-gather.23
  621.7 35.8 reduce-scatter.22
  659.9 37.5 reduce-scatter.24
  712.8 9.7 reduce-scatter.58
  724.8 31.8 reduce-scatter.38
  758.9 31.8 reduce-scatter.34
  792.8 31.8 reduce-scatter.26
  826.9 31.8 reduce-scatter.30
  860.9 54.3 reduce-scatter.54
  917.5 54.2 reduce-scatter.50
  974.1 99.2 reduce-scatter.42
  1075.6 99.2 reduce-scatter.46
  1178.9 55.0 reduce-scatter.60
  1237.7 56.4 reduce-scatter.40
  1298.2 56.3 reduce-scatter.36
  1358.1 56.4 reduce-scatter.28
  1418.7 56.3 reduce-scatter.32
  1478.7 60.5 reduce-scatter.56
  1543.3 60.5 reduce-scatter.52
  1607.8 71.5 reduce-scatter.44
  1683.8 71.3 reduce-scatter.48
